TPU v7x, 512 devices: a whole 4x8x8 slice. The times are simulated.
512 devices in a mesh: gx: 32 (over y_hi, z, core), yz: 16 (over x, y_lo).
Axes of the slice: x: 4, y: 8 (y_hi: 2, y_lo: 4; y = y_hi * 4 + y_lo), z: 8, core: 2. Of those that a mesh axis runs over, the one named last changes fastest.
Arguments:
- gauge_links: float32 [64, 2, 3, 3, 2048], P('gx', None, None, None, 'yz'), may hold values from -1 to 1, as said below
- in_field: float32 [8, 64, 2, 3, 3, 2048], P(None, 'gx', None, None, None, 'yz'), may hold values from -6 to 6
- cotangent: float32 [8, 64, 2, 3, 3, 2048], P(None, 'gx', None, None, None, 'yz'), may hold values from -6 to 6
- bilinear_weights: float32 [8, 8, 24, 8], replicated, may hold values from -0.15625 to 0.15625
Outputs:
- grad_field: float32 [8, 64, 2, 3, 3, 2048], P(None, 'gx', None, None, None, 'yz')
- grad_weights: float32 [8, 8, 24, 8], replicated
Inputs may be any that keep to these rules, and one draw needn't show every extreme that they name: `gauge_links`: every site's link is a special unitary 3 x 3 matrix (unitary with determinant 1), stored as real and imaginary parts.
All inputs are finite; a program needn't handle non-finite values.
Results may differ from a plain program's by a relative error of at most 0.0003.
Values sent between devices are 32-bit elements; how exact they have to be, the bound alone decides.
No kernel may reach another device: no remote copies, remote signals or barrier semaphores. Data moves between devices by JAX's collectives and lax.ppermute only.
A program may use at most 64 MiB of HBM per device.

v0:
```python
import math
import jax
import jax.numpy as jnp
from jax import lax
from jax.sharding import PartitionSpec as P


def from_behind(block, axis, distance):
    devices = range(lax.axis_size(axis))
    route = [((i - distance) % len(devices), i) for i in devices]
    return lax.ppermute(block, axis, route)


def matmul_three(left, right):
    return jnp.sum(left[..., :, :, None, :] * right[..., None, :, :, :], axis=-3)


def complex_mul(left, right):
    left_re = left[..., 0, :, :, :]
    left_im = left[..., 1, :, :, :]
    right_re = right[..., 0, :, :, :]
    right_im = right[..., 1, :, :, :]
    real_part = matmul_three(left_re, right_re) - matmul_three(left_im, right_im)
    imag_part = matmul_three(left_re, right_im) + matmul_three(left_im, right_re)
    return jnp.stack([real_part, imag_part], axis=-4)


def dagger(matrix):
    swapped = jnp.swapaxes(matrix, -3, -2)
    return jnp.stack([swapped[..., 0, :, :, :], -swapped[..., 1, :, :, :]], axis=-4)


def per_device(gauge_links, in_field, cotangent, bilinear_weights):
    part_x = gauge_links.shape[0]
    channels = in_field.shape[0]
    line_count = bilinear_weights.shape[2]
    site_count = gauge_links.shape[-1]
    reach_devs = (part_x - 1 + line_count) // part_x
    highest = lax.Precision.HIGHEST
    weight_rows = bilinear_weights.reshape(channels * channels, line_count * channels)

    def advance(carry, unused):
        arrived = from_behind(carry, "gx", -1)
        return (arrived, arrived)

    unused_last, stacked = lax.scan(advance, (gauge_links, in_field), None, length=reach_devs)
    window_links = jnp.concatenate(
        [gauge_links, stacked[0].reshape((-1, 2, 3, 3, site_count))], axis=0
    )
    later_field = jnp.moveaxis(stacked[1], 0, 1).reshape((channels, -1, 2, 3, 3, site_count))
    window_field = jnp.concatenate([in_field, later_field], axis=1)
    pair_grad = complex_mul(dagger(in_field)[None], cotangent[:, None]).reshape(
        channels * channels, -1
    )

    def forward_step(line, offset):
        shifted = lax.dynamic_slice_in_dim(window_field, offset, part_x, axis=1)
        transported = complex_mul(complex_mul(line[None], shifted), dagger(line)[None])
        next_links = lax.dynamic_slice_in_dim(window_links, offset, part_x, axis=0)
        return (complex_mul(line, next_links), (transported, line))

    offsets = jnp.arange(1, line_count + 1, dtype=jnp.int32)
    unused_line, (all_transported, all_lines) = lax.scan(forward_step, gauge_links, offsets)
    transported_flat = all_transported.reshape(line_count * channels, -1)
    partial_grad = lax.dot_general(
        pair_grad, transported_flat, (((1,), (1,)), ((), ())), precision=highest
    )
    mixed = jnp.dot(weight_rows, transported_flat, precision=highest)
    mixed_matrix = mixed.reshape((channels, channels) + in_field.shape[1:])
    direct = jnp.sum(complex_mul(cotangent[:, None], dagger(mixed_matrix)), axis=0)
    line_grad = jnp.dot(weight_rows.T, pair_grad, precision=highest)
    line_grad = line_grad.reshape((line_count,) + in_field.shape)
    accumulator = jnp.zeros((channels, (reach_devs + 1) * part_x, 2, 3, 3, site_count), jnp.float32)

    def backward_step(carry, inputs):
        offset, grad_piece, line = inputs
        contribution = complex_mul(complex_mul(dagger(line)[None], grad_piece), line[None])
        current = lax.dynamic_slice_in_dim(carry, offset, part_x, axis=1)
        return (
            lax.dynamic_update_slice_in_dim(carry, current + contribution, offset, axis=1),
            None,
        )

    accumulator, unused_out = lax.scan(backward_step, accumulator, (offsets, line_grad, all_lines))
    blocks = jnp.moveaxis(
        accumulator.reshape((channels, reach_devs + 1, part_x, 2, 3, 3, site_count)), 1, 0
    )

    def return_step(carry, block):
        arrived = from_behind(carry, "gx", 1)
        return (arrived + block, None)

    far_terms, unused_tail = lax.scan(return_step, blocks[reach_devs], blocks[:reach_devs][::-1])
    grad_field = direct + far_terms
    total_x = part_x * lax.axis_size("gx")
    total_sites = site_count * lax.axis_size("yz")
    summed = lax.psum(partial_grad, ("gx", "yz"))
    grad_weights = summed.reshape(channels, channels, line_count, channels) / math.sqrt(
        100.0 * total_x * total_sites
    )
    return (grad_field, grad_weights)


def solution(mesh):
    placed = (
        P("gx", None, None, None, "yz"),
        P(None, "gx", None, None, None, "yz"),
        P(None, "gx", None, None, None, "yz"),
        P(),
    )
    return jax.shard_map(
        per_device,
        mesh=mesh,
        in_specs=placed,
        out_specs=(P(None, "gx", None, None, None, "yz"), P()),
        check_vma=False,
    )
```

profile of v0, /device:TPU:2, one launch (start us, length us, event | category | flops | bytes accessed | tf_op | source)
XLA Modules:
  0.0 771.0 jit_solution(7964423564091880756)
XLA Ops:
  2.4 183.7 %while.50 = (s32[]{:T(128)}, f32[2,2,3,3,128]{4,1,3,2,0:T(2,128)S(1)}, f32[8,2,2,3,3,128]{5,2,4,3,1,0:T(2,128)S(1)}, f32[12,2,2,3,3,128]{5,1,0,4,3,2:T(2,128)S(1...) while((s32[]{:T(128)}, f32[2,2,3,3,128]{4,1,3,2,0:T(2,128)S(1)}, ...), condition=%wide.region_1.2_spmd, body=%wide.region_0.1_spmd.sunk | while | flops 2 | bytes 1327269 | solution.py:46
  2.4 15.6 %collective-permute-start = (f32[2,2,3,3,128]{4,1,3,2,0:T(2,128)S(1)}, f32[2,2,3,3,128]{4,1,3,2,0:T(2,128)S(1)}, u32[]{:S(2)}, u32[]{:S(2)}) collective-permute-start(f32[2,2,3,3,128]{4,1,3,2,0:T(2,128)S(1)} %get-tuple-element.507), channel_id=1, source_target_pairs={{16,0},{32,16},{48,32},{64,48},{80,64},{96,80},{112,96},{128,112},... | collective-permute-start | bytes 55304 | tf_op jit(solution)/shard_map/while/body/eval_jaxpr/ppermute | solution.py:11
  18.0 2.6 collective-permute-start.1
  20.6 4.2 collective-permute-done.1
  24.9 9.8 %collective-permute-start = (f32[2,2,3,3,128]{4,1,3,2,0:T(2,128)S(1)}, f32[2,2,3,3,128]{4,1,3,2,0:T(2,128)S(1)}, u32[]{:S(2)}, u32[]{:S(2)}) collective-permute-start(f32[2,2,3,3,128]{4,1,3,2,0:T(2,128)S(1)} %get-tuple-element.507), channel_id=1, source_target_pairs={{16,0},{32,16},{48,32},{64,48},{80,64},{96,80},{112,96},{128,112},... | collective-permute-start | bytes 55304 | tf_op jit(solution)/shard_map/while/body/eval_jaxpr/ppermute | solution.py:11
  34.7 1.9 collective-permute-start.1
  36.7 3.9 collective-permute-done.1
  40.8 9.8 %collective-permute-start = (f32[2,2,3,3,128]{4,1,3,2,0:T(2,128)S(1)}, f32[2,2,3,3,128]{4,1,3,2,0:T(2,128)S(1)}, u32[]{:S(2)}, u32[]{:S(2)}) collective-permute-start(f32[2,2,3,3,128]{4,1,3,2,0:T(2,128)S(1)} %get-tuple-element.507), channel_id=1, source_target_pairs={{16,0},{32,16},{48,32},{64,48},{80,64},{96,80},{112,96},{128,112},... | collective-permute-start | bytes 55304 | tf_op jit(solution)/shard_map/while/body/eval_jaxpr/ppermute | solution.py:11
  50.6 1.9 collective-permute-start.1
  52.6 2.7 collective-permute-done.1
  55.4 9.8 %collective-permute-start = (f32[2,2,3,3,128]{4,1,3,2,0:T(2,128)S(1)}, f32[2,2,3,3,128]{4,1,3,2,0:T(2,128)S(1)}, u32[]{:S(2)}, u32[]{:S(2)}) collective-permute-start(f32[2,2,3,3,128]{4,1,3,2,0:T(2,128)S(1)} %get-tuple-element.507), channel_id=1, source_target_pairs={{16,0},{32,16},{48,32},{64,48},{80,64},{96,80},{112,96},{128,112},... | collective-permute-start | bytes 55304 | tf_op jit(solution)/shard_map/while/body/eval_jaxpr/ppermute | solution.py:11
  65.2 1.9 collective-permute-start.1
  67.2 2.6 collective-permute-done.1
  69.9 9.8 %collective-permute-start = (f32[2,2,3,3,128]{4,1,3,2,0:T(2,128)S(1)}, f32[2,2,3,3,128]{4,1,3,2,0:T(2,128)S(1)}, u32[]{:S(2)}, u32[]{:S(2)}) collective-permute-start(f32[2,2,3,3,128]{4,1,3,2,0:T(2,128)S(1)} %get-tuple-element.507), channel_id=1, source_target_pairs={{16,0},{32,16},{48,32},{64,48},{80,64},{96,80},{112,96},{128,112},... | collective-permute-start | bytes 55304 | tf_op jit(solution)/shard_map/while/body/eval_jaxpr/ppermute | solution.py:11
  79.8 1.9 collective-permute-start.1
  81.7 2.6 collective-permute-done.1
  84.4 9.8 %collective-permute-start = (f32[2,2,3,3,128]{4,1,3,2,0:T(2,128)S(1)}, f32[2,2,3,3,128]{4,1,3,2,0:T(2,128)S(1)}, u32[]{:S(2)}, u32[]{:S(2)}) collective-permute-start(f32[2,2,3,3,128]{4,1,3,2,0:T(2,128)S(1)} %get-tuple-element.507), channel_id=1, source_target_pairs={{16,0},{32,16},{48,32},{64,48},{80,64},{96,80},{112,96},{128,112},... | collective-permute-start | bytes 55304 | tf_op jit(solution)/shard_map/while/body/eval_jaxpr/ppermute | solution.py:11
  94.3 1.9 collective-permute-start.1
  96.3 2.6 collective-permute-done.1
  99.0 9.8 %collective-permute-start = (f32[2,2,3,3,128]{4,1,3,2,0:T(2,128)S(1)}, f32[2,2,3,3,128]{4,1,3,2,0:T(2,128)S(1)}, u32[]{:S(2)}, u32[]{:S(2)}) collective-permute-start(f32[2,2,3,3,128]{4,1,3,2,0:T(2,128)S(1)} %get-tuple-element.507), channel_id=1, source_target_pairs={{16,0},{32,16},{48,32},{64,48},{80,64},{96,80},{112,96},{128,112},... | collective-permute-start | bytes 55304 | tf_op jit(solution)/shard_map/while/body/eval_jaxpr/ppermute | solution.py:11
  108.8 1.9 collective-permute-start.1
  110.8 2.6 collective-permute-done.1
  113.5 9.8 %collective-permute-start = (f32[2,2,3,3,128]{4,1,3,2,0:T(2,128)S(1)}, f32[2,2,3,3,128]{4,1,3,2,0:T(2,128)S(1)}, u32[]{:S(2)}, u32[]{:S(2)}) collective-permute-start(f32[2,2,3,3,128]{4,1,3,2,0:T(2,128)S(1)} %get-tuple-element.507), channel_id=1, source_target_pairs={{16,0},{32,16},{48,32},{64,48},{80,64},{96,80},{112,96},{128,112},... | collective-permute-start | bytes 55304 | tf_op jit(solution)/shard_map/while/body/eval_jaxpr/ppermute | solution.py:11
  123.3 1.9 collective-permute-start.1
  125.3 2.6 collective-permute-done.1
  128.0 9.8 %collective-permute-start = (f32[2,2,3,3,128]{4,1,3,2,0:T(2,128)S(1)}, f32[2,2,3,3,128]{4,1,3,2,0:T(2,128)S(1)}, u32[]{:S(2)}, u32[]{:S(2)}) collective-permute-start(f32[2,2,3,3,128]{4,1,3,2,0:T(2,128)S(1)} %get-tuple-element.507), channel_id=1, source_target_pairs={{16,0},{32,16},{48,32},{64,48},{80,64},{96,80},{112,96},{128,112},... | collective-permute-start | bytes 55304 | tf_op jit(solution)/shard_map/while/body/eval_jaxpr/ppermute | solution.py:11
  137.8 1.9 collective-permute-start.1
  139.8 2.6 collective-permute-done.1
  142.5 9.8 %collective-permute-start = (f32[2,2,3,3,128]{4,1,3,2,0:T(2,128)S(1)}, f32[2,2,3,3,128]{4,1,3,2,0:T(2,128)S(1)}, u32[]{:S(2)}, u32[]{:S(2)}) collective-permute-start(f32[2,2,3,3,128]{4,1,3,2,0:T(2,128)S(1)} %get-tuple-element.507), channel_id=1, source_target_pairs={{16,0},{32,16},{48,32},{64,48},{80,64},{96,80},{112,96},{128,112},... | collective-permute-start | bytes 55304 | tf_op jit(solution)/shard_map/while/body/eval_jaxpr/ppermute | solution.py:11
  152.3 1.9 collective-permute-start.1
  154.3 2.6 collective-permute-done.1
  157.0 9.8 %collective-permute-start = (f32[2,2,3,3,128]{4,1,3,2,0:T(2,128)S(1)}, f32[2,2,3,3,128]{4,1,3,2,0:T(2,128)S(1)}, u32[]{:S(2)}, u32[]{:S(2)}) collective-permute-start(f32[2,2,3,3,128]{4,1,3,2,0:T(2,128)S(1)} %get-tuple-element.507), channel_id=1, source_target_pairs={{16,0},{32,16},{48,32},{64,48},{80,64},{96,80},{112,96},{128,112},... | collective-permute-start | bytes 55304 | tf_op jit(solution)/shard_map/while/body/eval_jaxpr/ppermute | solution.py:11
  166.9 1.9 collective-permute-start.1
  168.9 2.6 collective-permute-done.1
  171.6 9.8 %collective-permute-start = (f32[2,2,3,3,128]{4,1,3,2,0:T(2,128)S(1)}, f32[2,2,3,3,128]{4,1,3,2,0:T(2,128)S(1)}, u32[]{:S(2)}, u32[]{:S(2)}) collective-permute-start(f32[2,2,3,3,128]{4,1,3,2,0:T(2,128)S(1)} %get-tuple-element.507), channel_id=1, source_target_pairs={{16,0},{32,16},{48,32},{64,48},{80,64},{96,80},{112,96},{128,112},... | collective-permute-start | bytes 55304 | tf_op jit(solution)/shard_map/while/body/eval_jaxpr/ppermute | solution.py:11
  181.4 1.9 collective-permute-start.1
  183.4 2.6 collective-permute-done.1
  189.8 184.4 %while.51 = (s32[]{:T(128)}, f32[2,2,3,3,128]{4,0,3,2,1:T(2,128)}, f32[24,8,2,2,3,3,128]{6,1,5,4,3,2,0:T(8,128)S(1)}, f32[24,2,2,3,3,128]{5,1,4,3,2,0:T(2,128)},...) while((s32[]{:T(128)}, f32[2,2,3,3,128]{4,0,3,2,1:T(2,128)}, ...), condition=%wide.region_15.16_spmd, body=%wide.region_2.15_spmd.sunk | while | flops 910086 | bytes 2968279 | solution.py:63
  374.2 2.1 copy.70
  376.3 2.0 reshape.184
  378.3 3.3 fusion.5
  382.8 3.8 multiply_reduce_fusion.27
  387.9 4.2 fusion.7
  392.1 100.0 %psum.7 = f32[64,192]{1,0:T(8,128)S(1)} all-reduce(f32[64,192]{1,0:T(8,128)} %fusion.7), channel_id=1, replica_groups=mesh['gx'=32,'yz'=16] {'gx','yz'}, use_global_device_ids=true, to_apply=%region_37.38 | all-reduce | flops 12288 | bytes 98304 | tf_op jit(solution)/shard_map/psum | solution.py:97
  493.3 4.7 fusion.6
  498.1 104.9 %while.52 = (s32[]{:T(128)}, f32[8,26,2,3,3,128]{5,0,4,3,2,1:T(8,128)S(1)}, s32[24]{0:T(128)S(1)}, f32[24,2,2,3,3,128]{5,1,4,3,2,0:T(2,128)}, f32[24,8,2,2,3,3,1...) while((s32[]{:T(128)}, f32[8,26,2,3,3,128]{5,0,4,3,2,1:T(8,128)S(1)}, s32[24]{0:T(128)S(1)}, ...), condition=%wide.region_34.35_spmd, body=%wide.region_25.34_spmd.sunk | while | flops 891653 | bytes 3411083 | solution.py:84
  604.4 2.9 rev.3
  607.3 161.5 %while.53 = (s32[]{:T(128)}, f32[8,2,2,3,3,128]{5,4,3,2,1,0:T(4,128)S(1)}, f32[12,8,2,2,3,3,128]{6,1,5,4,3,2,0:T(8,128)}, s32[]{:T(128)}) while((s32[]{:T(128)}, f32[8,2,2,3,3,128]{5,4,3,2,1,0:T(4,128)S(1)}, f32[12,8,2,2,3,3,128]{6,1,5,4,3,2,0:T(8,128)}, s32[]{:T(128)}) %tuple.163), condition=%wide.region_36.37_spmd, body=%wide.region_35.36_spmd.sunk | while | flops 36866 | bytes 1327209 | solution.py:93
  607.3 2.1 collective-permute-start.2
  610.3 12.3 %collective-permute-done.2 = f32[8,2,2,3,3,128]{5,4,3,2,1,0:T(4,128)S(1)} collective-permute-done((f32[8,2,2,3,3,128]{5,4,3,2,1,0:T(4,128)S(1)}, f32[8,2,2,3,3,128]{5,4,3,2,1,0:T(4,128)S(1)}, u32[]{:S(2)}, u32[]{:S(2)}) %collective-permute-start.2) | collective-permute-done | bytes 147488 | tf_op jit(solution)/shard_map/while/body/eval_jaxpr/ppermute | solution.py:11
  625.5 12.2 %collective-permute-done.2 = f32[8,2,2,3,3,128]{5,4,3,2,1,0:T(4,128)S(1)} collective-permute-done((f32[8,2,2,3,3,128]{5,4,3,2,1,0:T(4,128)S(1)}, f32[8,2,2,3,3,128]{5,4,3,2,1,0:T(4,128)S(1)}, u32[]{:S(2)}, u32[]{:S(2)}) %collective-permute-start.2) | collective-permute-done | bytes 147488 | tf_op jit(solution)/shard_map/while/body/eval_jaxpr/ppermute | solution.py:11
  640.7 10.2 %collective-permute-done.2 = f32[8,2,2,3,3,128]{5,4,3,2,1,0:T(4,128)S(1)} collective-permute-done((f32[8,2,2,3,3,128]{5,4,3,2,1,0:T(4,128)S(1)}, f32[8,2,2,3,3,128]{5,4,3,2,1,0:T(4,128)S(1)}, u32[]{:S(2)}, u32[]{:S(2)}) %collective-permute-start.2) | collective-permute-done | bytes 147488 | tf_op jit(solution)/shard_map/while/body/eval_jaxpr/ppermute | solution.py:11
  651.1 1.9 collective-permute-start.2
  653.9 10.2 %collective-permute-done.2 = f32[8,2,2,3,3,128]{5,4,3,2,1,0:T(4,128)S(1)} collective-permute-done((f32[8,2,2,3,3,128]{5,4,3,2,1,0:T(4,128)S(1)}, f32[8,2,2,3,3,128]{5,4,3,2,1,0:T(4,128)S(1)}, u32[]{:S(2)}, u32[]{:S(2)}) %collective-permute-start.2) | collective-permute-done | bytes 147488 | tf_op jit(solution)/shard_map/while/body/eval_jaxpr/ppermute | solution.py:11
  667.0 10.1 %collective-permute-done.2 = f32[8,2,2,3,3,128]{5,4,3,2,1,0:T(4,128)S(1)} collective-permute-done((f32[8,2,2,3,3,128]{5,4,3,2,1,0:T(4,128)S(1)}, f32[8,2,2,3,3,128]{5,4,3,2,1,0:T(4,128)S(1)}, u32[]{:S(2)}, u32[]{:S(2)}) %collective-permute-start.2) | collective-permute-done | bytes 147488 | tf_op jit(solution)/shard_map/while/body/eval_jaxpr/ppermute | solution.py:11
  677.2 1.9 collective-permute-start.2
  680.1 10.1 %collective-permute-done.2 = f32[8,2,2,3,3,128]{5,4,3,2,1,0:T(4,128)S(1)} collective-permute-done((f32[8,2,2,3,3,128]{5,4,3,2,1,0:T(4,128)S(1)}, f32[8,2,2,3,3,128]{5,4,3,2,1,0:T(4,128)S(1)}, u32[]{:S(2)}, u32[]{:S(2)}) %collective-permute-start.2) | collective-permute-done | bytes 147488 | tf_op jit(solution)/shard_map/while/body/eval_jaxpr/ppermute | solution.py:11
  693.2 10.1 %collective-permute-done.2 = f32[8,2,2,3,3,128]{5,4,3,2,1,0:T(4,128)S(1)} collective-permute-done((f32[8,2,2,3,3,128]{5,4,3,2,1,0:T(4,128)S(1)}, f32[8,2,2,3,3,128]{5,4,3,2,1,0:T(4,128)S(1)}, u32[]{:S(2)}, u32[]{:S(2)}) %collective-permute-start.2) | collective-permute-done | bytes 147488 | tf_op jit(solution)/shard_map/while/body/eval_jaxpr/ppermute | solution.py:11
  706.3 10.1 %collective-permute-done.2 = f32[8,2,2,3,3,128]{5,4,3,2,1,0:T(4,128)S(1)} collective-permute-done((f32[8,2,2,3,3,128]{5,4,3,2,1,0:T(4,128)S(1)}, f32[8,2,2,3,3,128]{5,4,3,2,1,0:T(4,128)S(1)}, u32[]{:S(2)}, u32[]{:S(2)}) %collective-permute-start.2) | collective-permute-done | bytes 147488 | tf_op jit(solution)/shard_map/while/body/eval_jaxpr/ppermute | solution.py:11
  719.4 10.1 %collective-permute-done.2 = f32[8,2,2,3,3,128]{5,4,3,2,1,0:T(4,128)S(1)} collective-permute-done((f32[8,2,2,3,3,128]{5,4,3,2,1,0:T(4,128)S(1)}, f32[8,2,2,3,3,128]{5,4,3,2,1,0:T(4,128)S(1)}, u32[]{:S(2)}, u32[]{:S(2)}) %collective-permute-start.2) | collective-permute-done | bytes 147488 | tf_op jit(solution)/shard_map/while/body/eval_jaxpr/ppermute | solution.py:11
  729.6 1.9 collective-permute-start.2
  732.5 10.1 %collective-permute-done.2 = f32[8,2,2,3,3,128]{5,4,3,2,1,0:T(4,128)S(1)} collective-permute-done((f32[8,2,2,3,3,128]{5,4,3,2,1,0:T(4,128)S(1)}, f32[8,2,2,3,3,128]{5,4,3,2,1,0:T(4,128)S(1)}, u32[]{:S(2)}, u32[]{:S(2)}) %collective-permute-start.2) | collective-permute-done | bytes 147488 | tf_op jit(solution)/shard_map/while/body/eval_jaxpr/ppermute | solution.py:11
  745.6 10.1 %collective-permute-done.2 = f32[8,2,2,3,3,128]{5,4,3,2,1,0:T(4,128)S(1)} collective-permute-done((f32[8,2,2,3,3,128]{5,4,3,2,1,0:T(4,128)S(1)}, f32[8,2,2,3,3,128]{5,4,3,2,1,0:T(4,128)S(1)}, u32[]{:S(2)}, u32[]{:S(2)}) %collective-permute-start.2) | collective-permute-done | bytes 147488 | tf_op jit(solution)/shard_map/while/body/eval_jaxpr/ppermute | solution.py:11
  758.7 10.1 %collective-permute-done.2 = f32[8,2,2,3,3,128]{5,4,3,2,1,0:T(4,128)S(1)} collective-permute-done((f32[8,2,2,3,3,128]{5,4,3,2,1,0:T(4,128)S(1)}, f32[8,2,2,3,3,128]{5,4,3,2,1,0:T(4,128)S(1)}, u32[]{:S(2)}, u32[]{:S(2)}) %collective-permute-start.2) | collective-permute-done | bytes 147488 | tf_op jit(solution)/shard_map/while/body/eval_jaxpr/ppermute | solution.py:11
  (1181 shorter events, 234.8 us)
Async XLA Ops:
  1.6 184.5 %copy-start.11 = (f32[2,2,3,3,128]{4,1,3,2,0:T(2,128)S(1)}, f32[2,2,3,3,128]{4,1,3,2,0:T(2,128)}, u32[]{:S(2)}) copy-start(f32[2,2,3,3,128]{4,1,3,2,0:T(2,128)} %param.12) | copy-start | bytes 55300
  2.4 18.2 %collective-permute-start = (f32[2,2,3,3,128]{4,1,3,2,0:T(2,128)S(1)}, f32[2,2,3,3,128]{4,1,3,2,0:T(2,128)S(1)}, u32[]{:S(2)}, u32[]{:S(2)}) collective-permute-start(f32[2,2,3,3,128]{4,1,3,2,0:T(2,128)S(1)} %get-tuple-element.507), channel_id=1, source_target_pairs={{16,0},{32,16},{48,32},{64,48},{80,64},{96,80},{112,96},{128,112},... | collective-permute-start | bytes 55304 | tf_op jit(solution)/shard_map/while/body/eval_jaxpr/ppermute | solution.py:11
  18.0 6.8 collective-permute-start.1
  24.9 11.7 %collective-permute-start = (f32[2,2,3,3,128]{4,1,3,2,0:T(2,128)S(1)}, f32[2,2,3,3,128]{4,1,3,2,0:T(2,128)S(1)}, u32[]{:S(2)}, u32[]{:S(2)}) collective-permute-start(f32[2,2,3,3,128]{4,1,3,2,0:T(2,128)S(1)} %get-tuple-element.507), channel_id=1, source_target_pairs={{16,0},{32,16},{48,32},{64,48},{80,64},{96,80},{112,96},{128,112},... | collective-permute-start | bytes 55304 | tf_op jit(solution)/shard_map/while/body/eval_jaxpr/ppermute | solution.py:11
  34.7 5.9 collective-permute-start.1
  40.8 11.8 %collective-permute-start = (f32[2,2,3,3,128]{4,1,3,2,0:T(2,128)S(1)}, f32[2,2,3,3,128]{4,1,3,2,0:T(2,128)S(1)}, u32[]{:S(2)}, u32[]{:S(2)}) collective-permute-start(f32[2,2,3,3,128]{4,1,3,2,0:T(2,128)S(1)} %get-tuple-element.507), channel_id=1, source_target_pairs={{16,0},{32,16},{48,32},{64,48},{80,64},{96,80},{112,96},{128,112},... | collective-permute-start | bytes 55304 | tf_op jit(solution)/shard_map/while/body/eval_jaxpr/ppermute | solution.py:11
  50.6 4.7 collective-permute-start.1
  55.4 11.8 %collective-permute-start = (f32[2,2,3,3,128]{4,1,3,2,0:T(2,128)S(1)}, f32[2,2,3,3,128]{4,1,3,2,0:T(2,128)S(1)}, u32[]{:S(2)}, u32[]{:S(2)}) collective-permute-start(f32[2,2,3,3,128]{4,1,3,2,0:T(2,128)S(1)} %get-tuple-element.507), channel_id=1, source_target_pairs={{16,0},{32,16},{48,32},{64,48},{80,64},{96,80},{112,96},{128,112},... | collective-permute-start | bytes 55304 | tf_op jit(solution)/shard_map/while/body/eval_jaxpr/ppermute | solution.py:11
  65.2 4.6 collective-permute-start.1
  69.9 11.8 %collective-permute-start = (f32[2,2,3,3,128]{4,1,3,2,0:T(2,128)S(1)}, f32[2,2,3,3,128]{4,1,3,2,0:T(2,128)S(1)}, u32[]{:S(2)}, u32[]{:S(2)}) collective-permute-start(f32[2,2,3,3,128]{4,1,3,2,0:T(2,128)S(1)} %get-tuple-element.507), channel_id=1, source_target_pairs={{16,0},{32,16},{48,32},{64,48},{80,64},{96,80},{112,96},{128,112},... | collective-permute-start | bytes 55304 | tf_op jit(solution)/shard_map/while/body/eval_jaxpr/ppermute | solution.py:11
  79.8 4.6 collective-permute-start.1
  84.4 11.8 %collective-permute-start = (f32[2,2,3,3,128]{4,1,3,2,0:T(2,128)S(1)}, f32[2,2,3,3,128]{4,1,3,2,0:T(2,128)S(1)}, u32[]{:S(2)}, u32[]{:S(2)}) collective-permute-start(f32[2,2,3,3,128]{4,1,3,2,0:T(2,128)S(1)} %get-tuple-element.507), channel_id=1, source_target_pairs={{16,0},{32,16},{48,32},{64,48},{80,64},{96,80},{112,96},{128,112},... | collective-permute-start | bytes 55304 | tf_op jit(solution)/shard_map/while/body/eval_jaxpr/ppermute | solution.py:11
  94.3 4.6 collective-permute-start.1
  99.0 11.8 %collective-permute-start = (f32[2,2,3,3,128]{4,1,3,2,0:T(2,128)S(1)}, f32[2,2,3,3,128]{4,1,3,2,0:T(2,128)S(1)}, u32[]{:S(2)}, u32[]{:S(2)}) collective-permute-start(f32[2,2,3,3,128]{4,1,3,2,0:T(2,128)S(1)} %get-tuple-element.507), channel_id=1, source_target_pairs={{16,0},{32,16},{48,32},{64,48},{80,64},{96,80},{112,96},{128,112},... | collective-permute-start | bytes 55304 | tf_op jit(solution)/shard_map/while/body/eval_jaxpr/ppermute | solution.py:11
  108.8 4.6 collective-permute-start.1
  113.5 11.8 %collective-permute-start = (f32[2,2,3,3,128]{4,1,3,2,0:T(2,128)S(1)}, f32[2,2,3,3,128]{4,1,3,2,0:T(2,128)S(1)}, u32[]{:S(2)}, u32[]{:S(2)}) collective-permute-start(f32[2,2,3,3,128]{4,1,3,2,0:T(2,128)S(1)} %get-tuple-element.507), channel_id=1, source_target_pairs={{16,0},{32,16},{48,32},{64,48},{80,64},{96,80},{112,96},{128,112},... | collective-permute-start | bytes 55304 | tf_op jit(solution)/shard_map/while/body/eval_jaxpr/ppermute | solution.py:11
  123.3 4.6 collective-permute-start.1
  128.0 11.8 %collective-permute-start = (f32[2,2,3,3,128]{4,1,3,2,0:T(2,128)S(1)}, f32[2,2,3,3,128]{4,1,3,2,0:T(2,128)S(1)}, u32[]{:S(2)}, u32[]{:S(2)}) collective-permute-start(f32[2,2,3,3,128]{4,1,3,2,0:T(2,128)S(1)} %get-tuple-element.507), channel_id=1, source_target_pairs={{16,0},{32,16},{48,32},{64,48},{80,64},{96,80},{112,96},{128,112},... | collective-permute-start | bytes 55304 | tf_op jit(solution)/shard_map/while/body/eval_jaxpr/ppermute | solution.py:11
  137.8 4.6 collective-permute-start.1
  142.5 11.8 %collective-permute-start = (f32[2,2,3,3,128]{4,1,3,2,0:T(2,128)S(1)}, f32[2,2,3,3,128]{4,1,3,2,0:T(2,128)S(1)}, u32[]{:S(2)}, u32[]{:S(2)}) collective-permute-start(f32[2,2,3,3,128]{4,1,3,2,0:T(2,128)S(1)} %get-tuple-element.507), channel_id=1, source_target_pairs={{16,0},{32,16},{48,32},{64,48},{80,64},{96,80},{112,96},{128,112},... | collective-permute-start | bytes 55304 | tf_op jit(solution)/shard_map/while/body/eval_jaxpr/ppermute | solution.py:11
  152.3 4.6 collective-permute-start.1
  157.0 11.8 %collective-permute-start = (f32[2,2,3,3,128]{4,1,3,2,0:T(2,128)S(1)}, f32[2,2,3,3,128]{4,1,3,2,0:T(2,128)S(1)}, u32[]{:S(2)}, u32[]{:S(2)}) collective-permute-start(f32[2,2,3,3,128]{4,1,3,2,0:T(2,128)S(1)} %get-tuple-element.507), channel_id=1, source_target_pairs={{16,0},{32,16},{48,32},{64,48},{80,64},{96,80},{112,96},{128,112},... | collective-permute-start | bytes 55304 | tf_op jit(solution)/shard_map/while/body/eval_jaxpr/ppermute | solution.py:11
  166.9 4.6 collective-permute-start.1
  171.6 11.8 %collective-permute-start = (f32[2,2,3,3,128]{4,1,3,2,0:T(2,128)S(1)}, f32[2,2,3,3,128]{4,1,3,2,0:T(2,128)S(1)}, u32[]{:S(2)}, u32[]{:S(2)}) collective-permute-start(f32[2,2,3,3,128]{4,1,3,2,0:T(2,128)S(1)} %get-tuple-element.507), channel_id=1, source_target_pairs={{16,0},{32,16},{48,32},{64,48},{80,64},{96,80},{112,96},{128,112},... | collective-permute-start | bytes 55304 | tf_op jit(solution)/shard_map/while/body/eval_jaxpr/ppermute | solution.py:11
  181.4 4.6 collective-permute-start.1
  192.5 2.7 copy-start.3
  200.2 2.7 copy-start.3
  207.9 2.7 copy-start.3
  215.6 2.7 copy-start.3
  223.2 2.7 copy-start.3
  230.9 2.7 copy-start.3
  238.6 2.7 copy-start.3
  246.3 2.7 copy-start.3
  254.0 2.7 copy-start.3
  261.7 2.7 copy-start.3
  269.4 2.7 copy-start.3
  277.1 2.7 copy-start.3
  284.8 2.7 copy-start.3
  292.4 2.7 copy-start.3
  300.1 2.7 copy-start.3
  307.8 2.7 copy-start.3
  315.5 2.7 copy-start.3
  323.2 2.7 copy-start.3
  330.9 2.7 copy-start.3
  338.6 2.7 copy-start.3
  346.3 2.7 copy-start.3
  353.9 2.7 copy-start.3
  392.1 101.2 %copy-start.1 = (f32[8,8,2,2,3,3,128]{6,1,5,4,3,2,0:T(8,128)S(1)}, f32[8,8,2,2,3,3,128]{6,1,5,4,3,2,0:T(8,128)}, u32[]{:S(2)}) copy-start(f32[8,8,2,2,3,3,128]{6,1,5,4,3,2,0:T(8,128)} %copy-done) | copy-start | bytes 3538948
  392.1 101.2 %copy-start.9 = (f32[64,192]{1,0:T(8,128)S(1)}, f32[64,192]{1,0:T(8,128)}, u32[]{:S(2)}) copy-start(f32[64,192]{1,0:T(8,128)} %reshape.184) | copy-start | bytes 147460
  604.4 164.5 %copy-start.6 = (f32[8,8,2,3,3,128]{5,1,4,3,2,0:T(8,128)S(1)}, f32[8,8,2,3,3,128]{5,1,4,3,2,0:T(8,128)}, u32[]{:S(2)}) copy-start(f32[8,8,2,3,3,128]{5,1,4,3,2,0:T(8,128)} %get-tuple-element.198) | copy-start | bytes 1769476
  607.2 161.6 %copy-start.5 = (f32[8,8,2,3,3,128]{5,1,4,3,2,0:T(8,128)S(1)}, f32[8,8,2,3,3,128]{5,1,4,3,2,0:T(8,128)}, u32[]{:S(2)}) copy-start(f32[8,8,2,3,3,128]{5,1,4,3,2,0:T(8,128)} %get-tuple-element.197) | copy-start | bytes 1769476
  607.3 161.6 %copy-start.4 = (f32[8,8,2,3,3,128]{5,1,4,3,2,0:T(8,128)S(1)}, f32[8,8,2,3,3,128]{5,1,4,3,2,0:T(8,128)}, u32[]{:S(2)}) copy-start(f32[8,8,2,3,3,128]{5,1,4,3,2,0:T(8,128)} %get-tuple-element.196) | copy-start | bytes 1769476
  607.3 15.2 %collective-permute-start.2 = (f32[8,2,2,3,3,128]{5,4,3,2,1,0:T(4,128)S(1)}, f32[8,2,2,3,3,128]{5,4,3,2,1,0:T(4,128)S(1)}, u32[]{:S(2)}, u32[]{:S(2)}) collective-permute-start(f32[8,2,2,3,3,128]{5,4,3,2,1,0:T(4,128)S(1)} %get-tuple-element.580), channel_id=1, source_target_pairs={{496,0},{0,16},{16,32},{32,48},{48,64},{64,80},{80,96},{96,112},{1... | collective-permute-start | bytes 442376 | tf_op jit(solution)/shard_map/while/body/eval_jaxpr/ppermute | solution.py:11
  622.7 15.1 %collective-permute-start.2 = (f32[8,2,2,3,3,128]{5,4,3,2,1,0:T(4,128)S(1)}, f32[8,2,2,3,3,128]{5,4,3,2,1,0:T(4,128)S(1)}, u32[]{:S(2)}, u32[]{:S(2)}) collective-permute-start(f32[8,2,2,3,3,128]{5,4,3,2,1,0:T(4,128)S(1)} %get-tuple-element.580), channel_id=1, source_target_pairs={{496,0},{0,16},{16,32},{32,48},{48,64},{64,80},{80,96},{96,112},{1... | collective-permute-start | bytes 442376 | tf_op jit(solution)/shard_map/while/body/eval_jaxpr/ppermute | solution.py:11
  637.9 13.1 %collective-permute-start.2 = (f32[8,2,2,3,3,128]{5,4,3,2,1,0:T(4,128)S(1)}, f32[8,2,2,3,3,128]{5,4,3,2,1,0:T(4,128)S(1)}, u32[]{:S(2)}, u32[]{:S(2)}) collective-permute-start(f32[8,2,2,3,3,128]{5,4,3,2,1,0:T(4,128)S(1)} %get-tuple-element.580), channel_id=1, source_target_pairs={{496,0},{0,16},{16,32},{32,48},{48,64},{64,80},{80,96},{96,112},{1... | collective-permute-start | bytes 442376 | tf_op jit(solution)/shard_map/while/body/eval_jaxpr/ppermute | solution.py:11
  651.1 13.0 %collective-permute-start.2 = (f32[8,2,2,3,3,128]{5,4,3,2,1,0:T(4,128)S(1)}, f32[8,2,2,3,3,128]{5,4,3,2,1,0:T(4,128)S(1)}, u32[]{:S(2)}, u32[]{:S(2)}) collective-permute-start(f32[8,2,2,3,3,128]{5,4,3,2,1,0:T(4,128)S(1)} %get-tuple-element.580), channel_id=1, source_target_pairs={{496,0},{0,16},{16,32},{32,48},{48,64},{64,80},{80,96},{96,112},{1... | collective-permute-start | bytes 442376 | tf_op jit(solution)/shard_map/while/body/eval_jaxpr/ppermute | solution.py:11
  664.2 13.0 %collective-permute-start.2 = (f32[8,2,2,3,3,128]{5,4,3,2,1,0:T(4,128)S(1)}, f32[8,2,2,3,3,128]{5,4,3,2,1,0:T(4,128)S(1)}, u32[]{:S(2)}, u32[]{:S(2)}) collective-permute-start(f32[8,2,2,3,3,128]{5,4,3,2,1,0:T(4,128)S(1)} %get-tuple-element.580), channel_id=1, source_target_pairs={{496,0},{0,16},{16,32},{32,48},{48,64},{64,80},{80,96},{96,112},{1... | collective-permute-start | bytes 442376 | tf_op jit(solution)/shard_map/while/body/eval_jaxpr/ppermute | solution.py:11
  677.2 13.0 %collective-permute-start.2 = (f32[8,2,2,3,3,128]{5,4,3,2,1,0:T(4,128)S(1)}, f32[8,2,2,3,3,128]{5,4,3,2,1,0:T(4,128)S(1)}, u32[]{:S(2)}, u32[]{:S(2)}) collective-permute-start(f32[8,2,2,3,3,128]{5,4,3,2,1,0:T(4,128)S(1)} %get-tuple-element.580), channel_id=1, source_target_pairs={{496,0},{0,16},{16,32},{32,48},{48,64},{64,80},{80,96},{96,112},{1... | collective-permute-start | bytes 442376 | tf_op jit(solution)/shard_map/while/body/eval_jaxpr/ppermute | solution.py:11
  690.3 13.0 %collective-permute-start.2 = (f32[8,2,2,3,3,128]{5,4,3,2,1,0:T(4,128)S(1)}, f32[8,2,2,3,3,128]{5,4,3,2,1,0:T(4,128)S(1)}, u32[]{:S(2)}, u32[]{:S(2)}) collective-permute-start(f32[8,2,2,3,3,128]{5,4,3,2,1,0:T(4,128)S(1)} %get-tuple-element.580), channel_id=1, source_target_pairs={{496,0},{0,16},{16,32},{32,48},{48,64},{64,80},{80,96},{96,112},{1... | collective-permute-start | bytes 442376 | tf_op jit(solution)/shard_map/while/body/eval_jaxpr/ppermute | solution.py:11
  703.4 13.0 %collective-permute-start.2 = (f32[8,2,2,3,3,128]{5,4,3,2,1,0:T(4,128)S(1)}, f32[8,2,2,3,3,128]{5,4,3,2,1,0:T(4,128)S(1)}, u32[]{:S(2)}, u32[]{:S(2)}) collective-permute-start(f32[8,2,2,3,3,128]{5,4,3,2,1,0:T(4,128)S(1)} %get-tuple-element.580), channel_id=1, source_target_pairs={{496,0},{0,16},{16,32},{32,48},{48,64},{64,80},{80,96},{96,112},{1... | collective-permute-start | bytes 442376 | tf_op jit(solution)/shard_map/while/body/eval_jaxpr/ppermute | solution.py:11
  716.5 13.0 %collective-permute-start.2 = (f32[8,2,2,3,3,128]{5,4,3,2,1,0:T(4,128)S(1)}, f32[8,2,2,3,3,128]{5,4,3,2,1,0:T(4,128)S(1)}, u32[]{:S(2)}, u32[]{:S(2)}) collective-permute-start(f32[8,2,2,3,3,128]{5,4,3,2,1,0:T(4,128)S(1)} %get-tuple-element.580), channel_id=1, source_target_pairs={{496,0},{0,16},{16,32},{32,48},{48,64},{64,80},{80,96},{96,112},{1... | collective-permute-start | bytes 442376 | tf_op jit(solution)/shard_map/while/body/eval_jaxpr/ppermute | solution.py:11
  729.6 13.0 %collective-permute-start.2 = (f32[8,2,2,3,3,128]{5,4,3,2,1,0:T(4,128)S(1)}, f32[8,2,2,3,3,128]{5,4,3,2,1,0:T(4,128)S(1)}, u32[]{:S(2)}, u32[]{:S(2)}) collective-permute-start(f32[8,2,2,3,3,128]{5,4,3,2,1,0:T(4,128)S(1)} %get-tuple-element.580), channel_id=1, source_target_pairs={{496,0},{0,16},{16,32},{32,48},{48,64},{64,80},{80,96},{96,112},{1... | collective-permute-start | bytes 442376 | tf_op jit(solution)/shard_map/while/body/eval_jaxpr/ppermute | solution.py:11
  742.7 13.0 %collective-permute-start.2 = (f32[8,2,2,3,3,128]{5,4,3,2,1,0:T(4,128)S(1)}, f32[8,2,2,3,3,128]{5,4,3,2,1,0:T(4,128)S(1)}, u32[]{:S(2)}, u32[]{:S(2)}) collective-permute-start(f32[8,2,2,3,3,128]{5,4,3,2,1,0:T(4,128)S(1)} %get-tuple-element.580), channel_id=1, source_target_pairs={{496,0},{0,16},{16,32},{32,48},{48,64},{64,80},{80,96},{96,112},{1... | collective-permute-start | bytes 442376 | tf_op jit(solution)/shard_map/while/body/eval_jaxpr/ppermute | solution.py:11
  755.8 13.0 %collective-permute-start.2 = (f32[8,2,2,3,3,128]{5,4,3,2,1,0:T(4,128)S(1)}, f32[8,2,2,3,3,128]{5,4,3,2,1,0:T(4,128)S(1)}, u32[]{:S(2)}, u32[]{:S(2)}) collective-permute-start(f32[8,2,2,3,3,128]{5,4,3,2,1,0:T(4,128)S(1)} %get-tuple-element.580), channel_id=1, source_target_pairs={{496,0},{0,16},{16,32},{32,48},{48,64},{64,80},{80,96},{96,112},{1... | collective-permute-start | bytes 442376 | tf_op jit(solution)/shard_map/while/body/eval_jaxpr/ppermute | solution.py:11
  (7 other events, 9.9 us)
where the time goes:
time: 780 us; the launch traced here: 771 us
  local copies, waits for them, and re-layouts  177 us (23%)
  starting transfers between devices  171 us (22%)
  waiting for transfers between devices  160 us (21%)
  blocking collectives  100 us (13%)
  loops' own time  96.8 us (12%)
  other arithmetic  53.1 us (7%)
  matrix products  12.2 us (2%)
    ppermute x36, starting transfers between devices, from_behind(): return lax.ppermute(block, axis, route)  171 us
    ppermute x36, waiting for transfers between devices, from_behind(): return lax.ppermute(block, axis, route)  160 us
    psum x1, blocking collectives, per_device(): summed = lax.psum(partial_grad, ('gx', 'yz'))  100 us
    mul x364, local copies, waits for them, and re-layouts, matmul_three(): left[..., :, :, None, :] * right[..., None, :, :, :]  64.4 us
    another operation x1, loops' own time, per_device(): lax.scan(forward_step, gauge_links, offsets)  51.7 us
    another operation x1, loops' own time, per_device(): lax.scan(backward_step, accumulator, (offsets, line_grad, all_lines))  44 us
    dynamic_slice x48, local copies, waits for them, and re-layouts, per_device(): lax.scan(forward_step, gauge_links, offsets)  29.5 us
    squeeze x24, local copies, waits for them, and re-layouts, per_device(): lax.scan(backward_step, accumulator, (offsets, line_grad, all_lines))  22.2 us
  transfers between devices with their start and end apart: 36, of which 24 were waited for; matrix products, arithmetic and copies ran while one was open for 1% of the time, Pallas kernels for 0%

commit v1 on v0

--- a/solution.py
+++ b/solution.py
@@ -3,6 +3,13 @@
 import jax.numpy as jnp
 from jax import lax
 from jax.sharding import PartitionSpec as P
+from jax.lax import psum
+
+
+def tables_trace(content):
+    local_out = psum(content, "yz")
+    arr_now = psum(local_out, "gx")
+    return arr_now
 
 
 def from_behind(block, axis, distance):
@@ -94,7 +101,7 @@
     grad_field = direct + far_terms
     total_x = part_x * lax.axis_size("gx")
     total_sites = site_count * lax.axis_size("yz")
-    summed = lax.psum(partial_grad, ("gx", "yz"))
+    summed = tables_trace(partial_grad)
     grad_weights = summed.reshape(channels, channels, line_count, channels) / math.sqrt(
         100.0 * total_x * total_sites
     )

time: 780 us -> 919 us (1.18)
  the two profiles are of different devices: /device:TPU:2 before, /device:TPU:32 now
where the time goes in v1:
time: 919 us; the launch traced here: 910 us
  blocking collectives  250 us (27%)
  local copies, waits for them, and re-layouts  177 us (19%)
  starting transfers between devices  165 us (18%)
  waiting for transfers between devices  155 us (17%)
  loops' own time  96.8 us (11%)
  other arithmetic  53.1 us (6%)
  matrix products  12.2 us (1%)
    psum x1, blocking collectives, tables_trace(): arr_now = psum(local_out, 'gx')  167 us
    ppermute x36, starting transfers between devices, from_behind(): return lax.ppermute(block, axis, route)  165 us
    ppermute x36, waiting for transfers between devices, from_behind(): return lax.ppermute(block, axis, route)  155 us
    psum x1, blocking collectives, tables_trace(): local_out = psum(content, 'yz')  83 us
    mul x364, local copies, waits for them, and re-layouts, matmul_three(): left[..., :, :, None, :] * right[..., None, :, :, :]  64.4 us
    another operation x1, loops' own time, per_device(): lax.scan(forward_step, gauge_links, offsets)  51.7 us
    another operation x1, loops' own time, per_device(): lax.scan(backward_step, accumulator, (offsets, line_grad, all_lines))  44 us
    dynamic_slice x48, local copies, waits for them, and re-layouts, per_device(): lax.scan(forward_step, gauge_links, offsets)  29.5 us
  transfers between devices with their start and end apart: 36, of which 24 were waited for; matrix products, arithmetic and copies ran while one was open for 1% of the time, Pallas kernels for 0%

profile of v1, /device:TPU:32, one launch (start us, length us, event | category | flops | bytes accessed | tf_op | source)
XLA Modules:
  0.0 910.1 jit_solution(8239738062650898560)
XLA Ops:
  2.4 175.2 %while.50 = (s32[]{:T(128)}, f32[2,2,3,3,128]{4,1,3,2,0:T(2,128)S(1)}, f32[8,2,2,3,3,128]{5,2,4,3,1,0:T(2,128)S(1)}, f32[12,2,2,3,3,128]{5,1,0,4,3,2:T(2,128)S(1...) while((s32[]{:T(128)}, f32[2,2,3,3,128]{4,1,3,2,0:T(2,128)S(1)}, ...), condition=%wide.region_1.2_spmd, body=%wide.region_0.1_spmd.sunk | while | flops 2 | bytes 1327269 | solution.py:53
  2.4 9.9 %collective-permute-start = (f32[2,2,3,3,128]{4,1,3,2,0:T(2,128)S(1)}, f32[2,2,3,3,128]{4,1,3,2,0:T(2,128)S(1)}, u32[]{:S(2)}, u32[]{:S(2)}) collective-permute-start(f32[2,2,3,3,128]{4,1,3,2,0:T(2,128)S(1)} %get-tuple-element.507), channel_id=1, source_target_pairs={{16,0},{32,16},{48,32},{64,48},{80,64},{96,80},{112,96},{128,112},... | collective-permute-start | bytes 55304 | tf_op jit(solution)/shard_map/while/body/eval_jaxpr/ppermute | solution.py:18
  12.3 2.6 collective-permute-start.1
  14.9 2.8 collective-permute-done.1
  17.9 9.8 %collective-permute-start = (f32[2,2,3,3,128]{4,1,3,2,0:T(2,128)S(1)}, f32[2,2,3,3,128]{4,1,3,2,0:T(2,128)S(1)}, u32[]{:S(2)}, u32[]{:S(2)}) collective-permute-start(f32[2,2,3,3,128]{4,1,3,2,0:T(2,128)S(1)} %get-tuple-element.507), channel_id=1, source_target_pairs={{16,0},{32,16},{48,32},{64,48},{80,64},{96,80},{112,96},{128,112},... | collective-permute-start | bytes 55304 | tf_op jit(solution)/shard_map/while/body/eval_jaxpr/ppermute | solution.py:18
  27.7 1.9 collective-permute-start.1
  29.6 2.6 collective-permute-done.1
  32.4 9.8 %collective-permute-start = (f32[2,2,3,3,128]{4,1,3,2,0:T(2,128)S(1)}, f32[2,2,3,3,128]{4,1,3,2,0:T(2,128)S(1)}, u32[]{:S(2)}, u32[]{:S(2)}) collective-permute-start(f32[2,2,3,3,128]{4,1,3,2,0:T(2,128)S(1)} %get-tuple-element.507), channel_id=1, source_target_pairs={{16,0},{32,16},{48,32},{64,48},{80,64},{96,80},{112,96},{128,112},... | collective-permute-start | bytes 55304 | tf_op jit(solution)/shard_map/while/body/eval_jaxpr/ppermute | solution.py:18
  42.2 1.9 collective-permute-start.1
  44.2 2.6 collective-permute-done.1
  46.9 9.8 %collective-permute-start = (f32[2,2,3,3,128]{4,1,3,2,0:T(2,128)S(1)}, f32[2,2,3,3,128]{4,1,3,2,0:T(2,128)S(1)}, u32[]{:S(2)}, u32[]{:S(2)}) collective-permute-start(f32[2,2,3,3,128]{4,1,3,2,0:T(2,128)S(1)} %get-tuple-element.507), channel_id=1, source_target_pairs={{16,0},{32,16},{48,32},{64,48},{80,64},{96,80},{112,96},{128,112},... | collective-permute-start | bytes 55304 | tf_op jit(solution)/shard_map/while/body/eval_jaxpr/ppermute | solution.py:18
  56.7 1.9 collective-permute-start.1
  58.7 2.6 collective-permute-done.1
  61.4 9.8 %collective-permute-start = (f32[2,2,3,3,128]{4,1,3,2,0:T(2,128)S(1)}, f32[2,2,3,3,128]{4,1,3,2,0:T(2,128)S(1)}, u32[]{:S(2)}, u32[]{:S(2)}) collective-permute-start(f32[2,2,3,3,128]{4,1,3,2,0:T(2,128)S(1)} %get-tuple-element.507), channel_id=1, source_target_pairs={{16,0},{32,16},{48,32},{64,48},{80,64},{96,80},{112,96},{128,112},... | collective-permute-start | bytes 55304 | tf_op jit(solution)/shard_map/while/body/eval_jaxpr/ppermute | solution.py:18
  71.2 1.9 collective-permute-start.1
  73.2 2.6 collective-permute-done.1
  75.9 9.8 %collective-permute-start = (f32[2,2,3,3,128]{4,1,3,2,0:T(2,128)S(1)}, f32[2,2,3,3,128]{4,1,3,2,0:T(2,128)S(1)}, u32[]{:S(2)}, u32[]{:S(2)}) collective-permute-start(f32[2,2,3,3,128]{4,1,3,2,0:T(2,128)S(1)} %get-tuple-element.507), channel_id=1, source_target_pairs={{16,0},{32,16},{48,32},{64,48},{80,64},{96,80},{112,96},{128,112},... | collective-permute-start | bytes 55304 | tf_op jit(solution)/shard_map/while/body/eval_jaxpr/ppermute | solution.py:18
  85.8 1.9 collective-permute-start.1
  87.7 2.6 collective-permute-done.1
  90.5 9.8 %collective-permute-start = (f32[2,2,3,3,128]{4,1,3,2,0:T(2,128)S(1)}, f32[2,2,3,3,128]{4,1,3,2,0:T(2,128)S(1)}, u32[]{:S(2)}, u32[]{:S(2)}) collective-permute-start(f32[2,2,3,3,128]{4,1,3,2,0:T(2,128)S(1)} %get-tuple-element.507), channel_id=1, source_target_pairs={{16,0},{32,16},{48,32},{64,48},{80,64},{96,80},{112,96},{128,112},... | collective-permute-start | bytes 55304 | tf_op jit(solution)/shard_map/while/body/eval_jaxpr/ppermute | solution.py:18
  100.3 1.9 collective-permute-start.1
  102.3 2.6 collective-permute-done.1
  105.0 9.8 %collective-permute-start = (f32[2,2,3,3,128]{4,1,3,2,0:T(2,128)S(1)}, f32[2,2,3,3,128]{4,1,3,2,0:T(2,128)S(1)}, u32[]{:S(2)}, u32[]{:S(2)}) collective-permute-start(f32[2,2,3,3,128]{4,1,3,2,0:T(2,128)S(1)} %get-tuple-element.507), channel_id=1, source_target_pairs={{16,0},{32,16},{48,32},{64,48},{80,64},{96,80},{112,96},{128,112},... | collective-permute-start | bytes 55304 | tf_op jit(solution)/shard_map/while/body/eval_jaxpr/ppermute | solution.py:18
  116.8 2.6 collective-permute-done.1
  119.5 9.8 %collective-permute-start = (f32[2,2,3,3,128]{4,1,3,2,0:T(2,128)S(1)}, f32[2,2,3,3,128]{4,1,3,2,0:T(2,128)S(1)}, u32[]{:S(2)}, u32[]{:S(2)}) collective-permute-start(f32[2,2,3,3,128]{4,1,3,2,0:T(2,128)S(1)} %get-tuple-element.507), channel_id=1, source_target_pairs={{16,0},{32,16},{48,32},{64,48},{80,64},{96,80},{112,96},{128,112},... | collective-permute-start | bytes 55304 | tf_op jit(solution)/shard_map/while/body/eval_jaxpr/ppermute | solution.py:18
  129.3 1.9 collective-permute-start.1
  131.3 2.6 collective-permute-done.1
  134.0 9.8 %collective-permute-start = (f32[2,2,3,3,128]{4,1,3,2,0:T(2,128)S(1)}, f32[2,2,3,3,128]{4,1,3,2,0:T(2,128)S(1)}, u32[]{:S(2)}, u32[]{:S(2)}) collective-permute-start(f32[2,2,3,3,128]{4,1,3,2,0:T(2,128)S(1)} %get-tuple-element.507), channel_id=1, source_target_pairs={{16,0},{32,16},{48,32},{64,48},{80,64},{96,80},{112,96},{128,112},... | collective-permute-start | bytes 55304 | tf_op jit(solution)/shard_map/while/body/eval_jaxpr/ppermute | solution.py:18
  145.8 2.6 collective-permute-done.1
  148.5 9.8 %collective-permute-start = (f32[2,2,3,3,128]{4,1,3,2,0:T(2,128)S(1)}, f32[2,2,3,3,128]{4,1,3,2,0:T(2,128)S(1)}, u32[]{:S(2)}, u32[]{:S(2)}) collective-permute-start(f32[2,2,3,3,128]{4,1,3,2,0:T(2,128)S(1)} %get-tuple-element.507), channel_id=1, source_target_pairs={{16,0},{32,16},{48,32},{64,48},{80,64},{96,80},{112,96},{128,112},... | collective-permute-start | bytes 55304 | tf_op jit(solution)/shard_map/while/body/eval_jaxpr/ppermute | solution.py:18
  160.3 2.6 collective-permute-done.1
  163.1 9.8 %collective-permute-start = (f32[2,2,3,3,128]{4,1,3,2,0:T(2,128)S(1)}, f32[2,2,3,3,128]{4,1,3,2,0:T(2,128)S(1)}, u32[]{:S(2)}, u32[]{:S(2)}) collective-permute-start(f32[2,2,3,3,128]{4,1,3,2,0:T(2,128)S(1)} %get-tuple-element.507), channel_id=1, source_target_pairs={{16,0},{32,16},{48,32},{64,48},{80,64},{96,80},{112,96},{128,112},... | collective-permute-start | bytes 55304 | tf_op jit(solution)/shard_map/while/body/eval_jaxpr/ppermute | solution.py:18
  172.9 1.9 collective-permute-start.1
  174.9 2.6 collective-permute-done.1
  181.3 184.4 %while.51 = (s32[]{:T(128)}, f32[2,2,3,3,128]{4,0,3,2,1:T(2,128)}, f32[24,8,2,2,3,3,128]{6,1,5,4,3,2,0:T(8,128)S(1)}, f32[24,2,2,3,3,128]{5,1,4,3,2,0:T(2,128)},...) while((s32[]{:T(128)}, f32[2,2,3,3,128]{4,0,3,2,1:T(2,128)}, ...), condition=%wide.region_15.16_spmd, body=%wide.region_2.15_spmd.sunk | while | flops 910086 | bytes 2968279 | solution.py:70
  365.7 2.1 copy.70
  367.8 2.0 reshape.184
  369.8 3.3 fusion.5
  374.3 3.8 multiply_reduce_fusion.27
  379.4 4.2 fusion.7
  383.5 83.0 %psum.14 = f32[64,192]{1,0:T(8,128)S(1)} all-reduce(f32[64,192]{1,0:T(8,128)} %fusion.7), channel_id=1, replica_groups=mesh['gx'=32,'yz'=16] {'yz'}, use_global_device_ids=true, to_apply=%region_37.38 | all-reduce | flops 12288 | bytes 98304 | tf_op jit(solution)/shard_map/psum | solution.py:10
  466.6 167.1 %psum.15 = f32[64,192]{1,0:T(8,128)S(1)} all-reduce(f32[64,192]{1,0:T(8,128)S(1)} %psum.14), channel_id=1, replica_groups=mesh['gx'=32,'yz'=16] {'gx'}, use_global_device_ids=true, to_apply=%region_38.39 | all-reduce | flops 12288 | bytes 98304 | tf_op jit(solution)/shard_map/psum | solution.py:11
  635.0 4.7 fusion.6
  639.8 104.9 %while.52 = (s32[]{:T(128)}, f32[8,26,2,3,3,128]{5,0,4,3,2,1:T(8,128)S(1)}, s32[24]{0:T(128)S(1)}, f32[24,2,2,3,3,128]{5,1,4,3,2,0:T(2,128)}, f32[24,8,2,2,3,3,1...) while((s32[]{:T(128)}, f32[8,26,2,3,3,128]{5,0,4,3,2,1:T(8,128)S(1)}, s32[24]{0:T(128)S(1)}, ...), condition=%wide.region_34.35_spmd, body=%wide.region_25.34_spmd.sunk | while | flops 891653 | bytes 3411083 | solution.py:91
  746.0 2.9 rev.3
  749.0 159.1 %while.53 = (s32[]{:T(128)}, f32[8,2,2,3,3,128]{5,4,3,2,1,0:T(4,128)S(1)}, f32[12,8,2,2,3,3,128]{6,1,5,4,3,2,0:T(8,128)}, s32[]{:T(128)}) while((s32[]{:T(128)}, f32[8,2,2,3,3,128]{5,4,3,2,1,0:T(4,128)S(1)}, f32[12,8,2,2,3,3,128]{6,1,5,4,3,2,0:T(8,128)}, s32[]{:T(128)}) %tuple.163), condition=%wide.region_36.37_spmd, body=%wide.region_35.36_spmd.sunk | while | flops 36866 | bytes 1327209 | solution.py:100
  749.0 2.1 collective-permute-start.2
  752.0 11.9 %collective-permute-done.2 = f32[8,2,2,3,3,128]{5,4,3,2,1,0:T(4,128)S(1)} collective-permute-done((f32[8,2,2,3,3,128]{5,4,3,2,1,0:T(4,128)S(1)}, f32[8,2,2,3,3,128]{5,4,3,2,1,0:T(4,128)S(1)}, u32[]{:S(2)}, u32[]{:S(2)}) %collective-permute-start.2) | collective-permute-done | bytes 147488 | tf_op jit(solution)/shard_map/while/body/eval_jaxpr/ppermute | solution.py:18
  766.8 10.2 %collective-permute-done.2 = f32[8,2,2,3,3,128]{5,4,3,2,1,0:T(4,128)S(1)} collective-permute-done((f32[8,2,2,3,3,128]{5,4,3,2,1,0:T(4,128)S(1)}, f32[8,2,2,3,3,128]{5,4,3,2,1,0:T(4,128)S(1)}, u32[]{:S(2)}, u32[]{:S(2)}) %collective-permute-start.2) | collective-permute-done | bytes 147488 | tf_op jit(solution)/shard_map/while/body/eval_jaxpr/ppermute | solution.py:18
  777.1 1.9 collective-permute-start.2
  780.0 10.2 %collective-permute-done.2 = f32[8,2,2,3,3,128]{5,4,3,2,1,0:T(4,128)S(1)} collective-permute-done((f32[8,2,2,3,3,128]{5,4,3,2,1,0:T(4,128)S(1)}, f32[8,2,2,3,3,128]{5,4,3,2,1,0:T(4,128)S(1)}, u32[]{:S(2)}, u32[]{:S(2)}) %collective-permute-start.2) | collective-permute-done | bytes 147488 | tf_op jit(solution)/shard_map/while/body/eval_jaxpr/ppermute | solution.py:18
  793.1 10.1 %collective-permute-done.2 = f32[8,2,2,3,3,128]{5,4,3,2,1,0:T(4,128)S(1)} collective-permute-done((f32[8,2,2,3,3,128]{5,4,3,2,1,0:T(4,128)S(1)}, f32[8,2,2,3,3,128]{5,4,3,2,1,0:T(4,128)S(1)}, u32[]{:S(2)}, u32[]{:S(2)}) %collective-permute-start.2) | collective-permute-done | bytes 147488 | tf_op jit(solution)/shard_map/while/body/eval_jaxpr/ppermute | solution.py:18
  803.3 1.9 collective-permute-start.2
  806.2 10.1 %collective-permute-done.2 = f32[8,2,2,3,3,128]{5,4,3,2,1,0:T(4,128)S(1)} collective-permute-done((f32[8,2,2,3,3,128]{5,4,3,2,1,0:T(4,128)S(1)}, f32[8,2,2,3,3,128]{5,4,3,2,1,0:T(4,128)S(1)}, u32[]{:S(2)}, u32[]{:S(2)}) %collective-permute-start.2) | collective-permute-done | bytes 147488 | tf_op jit(solution)/shard_map/while/body/eval_jaxpr/ppermute | solution.py:18
  819.3 10.1 %collective-permute-done.2 = f32[8,2,2,3,3,128]{5,4,3,2,1,0:T(4,128)S(1)} collective-permute-done((f32[8,2,2,3,3,128]{5,4,3,2,1,0:T(4,128)S(1)}, f32[8,2,2,3,3,128]{5,4,3,2,1,0:T(4,128)S(1)}, u32[]{:S(2)}, u32[]{:S(2)}) %collective-permute-start.2) | collective-permute-done | bytes 147488 | tf_op jit(solution)/shard_map/while/body/eval_jaxpr/ppermute | solution.py:18
  832.4 10.1 %collective-permute-done.2 = f32[8,2,2,3,3,128]{5,4,3,2,1,0:T(4,128)S(1)} collective-permute-done((f32[8,2,2,3,3,128]{5,4,3,2,1,0:T(4,128)S(1)}, f32[8,2,2,3,3,128]{5,4,3,2,1,0:T(4,128)S(1)}, u32[]{:S(2)}, u32[]{:S(2)}) %collective-permute-start.2) | collective-permute-done | bytes 147488 | tf_op jit(solution)/shard_map/while/body/eval_jaxpr/ppermute | solution.py:18
  842.6 1.9 collective-permute-start.2
  845.5 10.1 %collective-permute-done.2 = f32[8,2,2,3,3,128]{5,4,3,2,1,0:T(4,128)S(1)} collective-permute-done((f32[8,2,2,3,3,128]{5,4,3,2,1,0:T(4,128)S(1)}, f32[8,2,2,3,3,128]{5,4,3,2,1,0:T(4,128)S(1)}, u32[]{:S(2)}, u32[]{:S(2)}) %collective-permute-start.2) | collective-permute-done | bytes 147488 | tf_op jit(solution)/shard_map/while/body/eval_jaxpr/ppermute | solution.py:18
  855.7 1.9 collective-permute-start.2
  858.5 10.1 %collective-permute-done.2 = f32[8,2,2,3,3,128]{5,4,3,2,1,0:T(4,128)S(1)} collective-permute-done((f32[8,2,2,3,3,128]{5,4,3,2,1,0:T(4,128)S(1)}, f32[8,2,2,3,3,128]{5,4,3,2,1,0:T(4,128)S(1)}, u32[]{:S(2)}, u32[]{:S(2)}) %collective-permute-start.2) | collective-permute-done | bytes 147488 | tf_op jit(solution)/shard_map/while/body/eval_jaxpr/ppermute | solution.py:18
  871.6 10.1 %collective-permute-done.2 = f32[8,2,2,3,3,128]{5,4,3,2,1,0:T(4,128)S(1)} collective-permute-done((f32[8,2,2,3,3,128]{5,4,3,2,1,0:T(4,128)S(1)}, f32[8,2,2,3,3,128]{5,4,3,2,1,0:T(4,128)S(1)}, u32[]{:S(2)}, u32[]{:S(2)}) %collective-permute-start.2) | collective-permute-done | bytes 147488 | tf_op jit(solution)/shard_map/while/body/eval_jaxpr/ppermute | solution.py:18
  884.7 10.1 %collective-permute-done.2 = f32[8,2,2,3,3,128]{5,4,3,2,1,0:T(4,128)S(1)} collective-permute-done((f32[8,2,2,3,3,128]{5,4,3,2,1,0:T(4,128)S(1)}, f32[8,2,2,3,3,128]{5,4,3,2,1,0:T(4,128)S(1)}, u32[]{:S(2)}, u32[]{:S(2)}) %collective-permute-start.2) | collective-permute-done | bytes 147488 | tf_op jit(solution)/shard_map/while/body/eval_jaxpr/ppermute | solution.py:18
  895.0 1.9 collective-permute-start.2
  897.8 10.1 %collective-permute-done.2 = f32[8,2,2,3,3,128]{5,4,3,2,1,0:T(4,128)S(1)} collective-permute-done((f32[8,2,2,3,3,128]{5,4,3,2,1,0:T(4,128)S(1)}, f32[8,2,2,3,3,128]{5,4,3,2,1,0:T(4,128)S(1)}, u32[]{:S(2)}, u32[]{:S(2)}) %collective-permute-start.2) | collective-permute-done | bytes 147488 | tf_op jit(solution)/shard_map/while/body/eval_jaxpr/ppermute | solution.py:18
  (1182 shorter events, 236.8 us)
Async XLA Ops:
  1.6 176.0 %copy-start.11 = (f32[2,2,3,3,128]{4,1,3,2,0:T(2,128)S(1)}, f32[2,2,3,3,128]{4,1,3,2,0:T(2,128)}, u32[]{:S(2)}) copy-start(f32[2,2,3,3,128]{4,1,3,2,0:T(2,128)} %param.12) | copy-start | bytes 55300
  2.4 12.5 %collective-permute-start = (f32[2,2,3,3,128]{4,1,3,2,0:T(2,128)S(1)}, f32[2,2,3,3,128]{4,1,3,2,0:T(2,128)S(1)}, u32[]{:S(2)}, u32[]{:S(2)}) collective-permute-start(f32[2,2,3,3,128]{4,1,3,2,0:T(2,128)S(1)} %get-tuple-element.507), channel_id=1, source_target_pairs={{16,0},{32,16},{48,32},{64,48},{80,64},{96,80},{112,96},{128,112},... | collective-permute-start | bytes 55304 | tf_op jit(solution)/shard_map/while/body/eval_jaxpr/ppermute | solution.py:18
  12.3 5.5 collective-permute-start.1
  17.9 11.7 %collective-permute-start = (f32[2,2,3,3,128]{4,1,3,2,0:T(2,128)S(1)}, f32[2,2,3,3,128]{4,1,3,2,0:T(2,128)S(1)}, u32[]{:S(2)}, u32[]{:S(2)}) collective-permute-start(f32[2,2,3,3,128]{4,1,3,2,0:T(2,128)S(1)} %get-tuple-element.507), channel_id=1, source_target_pairs={{16,0},{32,16},{48,32},{64,48},{80,64},{96,80},{112,96},{128,112},... | collective-permute-start | bytes 55304 | tf_op jit(solution)/shard_map/while/body/eval_jaxpr/ppermute | solution.py:18
  27.7 4.6 collective-permute-start.1
  32.4 11.8 %collective-permute-start = (f32[2,2,3,3,128]{4,1,3,2,0:T(2,128)S(1)}, f32[2,2,3,3,128]{4,1,3,2,0:T(2,128)S(1)}, u32[]{:S(2)}, u32[]{:S(2)}) collective-permute-start(f32[2,2,3,3,128]{4,1,3,2,0:T(2,128)S(1)} %get-tuple-element.507), channel_id=1, source_target_pairs={{16,0},{32,16},{48,32},{64,48},{80,64},{96,80},{112,96},{128,112},... | collective-permute-start | bytes 55304 | tf_op jit(solution)/shard_map/while/body/eval_jaxpr/ppermute | solution.py:18
  42.2 4.6 collective-permute-start.1
  46.9 11.8 %collective-permute-start = (f32[2,2,3,3,128]{4,1,3,2,0:T(2,128)S(1)}, f32[2,2,3,3,128]{4,1,3,2,0:T(2,128)S(1)}, u32[]{:S(2)}, u32[]{:S(2)}) collective-permute-start(f32[2,2,3,3,128]{4,1,3,2,0:T(2,128)S(1)} %get-tuple-element.507), channel_id=1, source_target_pairs={{16,0},{32,16},{48,32},{64,48},{80,64},{96,80},{112,96},{128,112},... | collective-permute-start | bytes 55304 | tf_op jit(solution)/shard_map/while/body/eval_jaxpr/ppermute | solution.py:18
  56.7 4.6 collective-permute-start.1
  61.4 11.8 %collective-permute-start = (f32[2,2,3,3,128]{4,1,3,2,0:T(2,128)S(1)}, f32[2,2,3,3,128]{4,1,3,2,0:T(2,128)S(1)}, u32[]{:S(2)}, u32[]{:S(2)}) collective-permute-start(f32[2,2,3,3,128]{4,1,3,2,0:T(2,128)S(1)} %get-tuple-element.507), channel_id=1, source_target_pairs={{16,0},{32,16},{48,32},{64,48},{80,64},{96,80},{112,96},{128,112},... | collective-permute-start | bytes 55304 | tf_op jit(solution)/shard_map/while/body/eval_jaxpr/ppermute | solution.py:18
  71.2 4.6 collective-permute-start.1
  75.9 11.8 %collective-permute-start = (f32[2,2,3,3,128]{4,1,3,2,0:T(2,128)S(1)}, f32[2,2,3,3,128]{4,1,3,2,0:T(2,128)S(1)}, u32[]{:S(2)}, u32[]{:S(2)}) collective-permute-start(f32[2,2,3,3,128]{4,1,3,2,0:T(2,128)S(1)} %get-tuple-element.507), channel_id=1, source_target_pairs={{16,0},{32,16},{48,32},{64,48},{80,64},{96,80},{112,96},{128,112},... | collective-permute-start | bytes 55304 | tf_op jit(solution)/shard_map/while/body/eval_jaxpr/ppermute | solution.py:18
  85.8 4.6 collective-permute-start.1
  90.5 11.8 %collective-permute-start = (f32[2,2,3,3,128]{4,1,3,2,0:T(2,128)S(1)}, f32[2,2,3,3,128]{4,1,3,2,0:T(2,128)S(1)}, u32[]{:S(2)}, u32[]{:S(2)}) collective-permute-start(f32[2,2,3,3,128]{4,1,3,2,0:T(2,128)S(1)} %get-tuple-element.507), channel_id=1, source_target_pairs={{16,0},{32,16},{48,32},{64,48},{80,64},{96,80},{112,96},{128,112},... | collective-permute-start | bytes 55304 | tf_op jit(solution)/shard_map/while/body/eval_jaxpr/ppermute | solution.py:18
  100.3 4.6 collective-permute-start.1
  105.0 11.8 %collective-permute-start = (f32[2,2,3,3,128]{4,1,3,2,0:T(2,128)S(1)}, f32[2,2,3,3,128]{4,1,3,2,0:T(2,128)S(1)}, u32[]{:S(2)}, u32[]{:S(2)}) collective-permute-start(f32[2,2,3,3,128]{4,1,3,2,0:T(2,128)S(1)} %get-tuple-element.507), channel_id=1, source_target_pairs={{16,0},{32,16},{48,32},{64,48},{80,64},{96,80},{112,96},{128,112},... | collective-permute-start | bytes 55304 | tf_op jit(solution)/shard_map/while/body/eval_jaxpr/ppermute | solution.py:18
  114.8 4.6 collective-permute-start.1
  119.5 11.8 %collective-permute-start = (f32[2,2,3,3,128]{4,1,3,2,0:T(2,128)S(1)}, f32[2,2,3,3,128]{4,1,3,2,0:T(2,128)S(1)}, u32[]{:S(2)}, u32[]{:S(2)}) collective-permute-start(f32[2,2,3,3,128]{4,1,3,2,0:T(2,128)S(1)} %get-tuple-element.507), channel_id=1, source_target_pairs={{16,0},{32,16},{48,32},{64,48},{80,64},{96,80},{112,96},{128,112},... | collective-permute-start | bytes 55304 | tf_op jit(solution)/shard_map/while/body/eval_jaxpr/ppermute | solution.py:18
  129.3 4.6 collective-permute-start.1
  134.0 11.8 %collective-permute-start = (f32[2,2,3,3,128]{4,1,3,2,0:T(2,128)S(1)}, f32[2,2,3,3,128]{4,1,3,2,0:T(2,128)S(1)}, u32[]{:S(2)}, u32[]{:S(2)}) collective-permute-start(f32[2,2,3,3,128]{4,1,3,2,0:T(2,128)S(1)} %get-tuple-element.507), channel_id=1, source_target_pairs={{16,0},{32,16},{48,32},{64,48},{80,64},{96,80},{112,96},{128,112},... | collective-permute-start | bytes 55304 | tf_op jit(solution)/shard_map/while/body/eval_jaxpr/ppermute | solution.py:18
  143.8 4.6 collective-permute-start.1
  148.5 11.8 %collective-permute-start = (f32[2,2,3,3,128]{4,1,3,2,0:T(2,128)S(1)}, f32[2,2,3,3,128]{4,1,3,2,0:T(2,128)S(1)}, u32[]{:S(2)}, u32[]{:S(2)}) collective-permute-start(f32[2,2,3,3,128]{4,1,3,2,0:T(2,128)S(1)} %get-tuple-element.507), channel_id=1, source_target_pairs={{16,0},{32,16},{48,32},{64,48},{80,64},{96,80},{112,96},{128,112},... | collective-permute-start | bytes 55304 | tf_op jit(solution)/shard_map/while/body/eval_jaxpr/ppermute | solution.py:18
  158.4 4.6 collective-permute-start.1
  163.1 11.8 %collective-permute-start = (f32[2,2,3,3,128]{4,1,3,2,0:T(2,128)S(1)}, f32[2,2,3,3,128]{4,1,3,2,0:T(2,128)S(1)}, u32[]{:S(2)}, u32[]{:S(2)}) collective-permute-start(f32[2,2,3,3,128]{4,1,3,2,0:T(2,128)S(1)} %get-tuple-element.507), channel_id=1, source_target_pairs={{16,0},{32,16},{48,32},{64,48},{80,64},{96,80},{112,96},{128,112},... | collective-permute-start | bytes 55304 | tf_op jit(solution)/shard_map/while/body/eval_jaxpr/ppermute | solution.py:18
  172.9 4.6 collective-permute-start.1
  184.0 2.7 copy-start.3
  191.7 2.7 copy-start.3
  199.4 2.7 copy-start.3
  207.0 2.7 copy-start.3
  214.7 2.7 copy-start.3
  222.4 2.7 copy-start.3
  230.1 2.7 copy-start.3
  237.8 2.7 copy-start.3
  245.5 2.7 copy-start.3
  253.2 2.7 copy-start.3
  260.9 2.7 copy-start.3
  268.6 2.7 copy-start.3
  276.3 2.7 copy-start.3
  283.9 2.7 copy-start.3
  291.6 2.7 copy-start.3
  299.3 2.7 copy-start.3
  307.0 2.7 copy-start.3
  314.7 2.7 copy-start.3
  322.4 2.7 copy-start.3
  330.1 2.7 copy-start.3
  337.8 2.7 copy-start.3
  345.4 2.7 copy-start.3
  383.5 251.4 %copy-start.1 = (f32[8,8,2,2,3,3,128]{6,1,5,4,3,2,0:T(8,128)S(1)}, f32[8,8,2,2,3,3,128]{6,1,5,4,3,2,0:T(8,128)}, u32[]{:S(2)}) copy-start(f32[8,8,2,2,3,3,128]{6,1,5,4,3,2,0:T(8,128)} %copy-done) | copy-start | bytes 3538948
  383.5 251.4 %copy-start.9 = (f32[64,192]{1,0:T(8,128)S(1)}, f32[64,192]{1,0:T(8,128)}, u32[]{:S(2)}) copy-start(f32[64,192]{1,0:T(8,128)} %reshape.184) | copy-start | bytes 147460
  746.0 162.0 %copy-start.6 = (f32[8,8,2,3,3,128]{5,1,4,3,2,0:T(8,128)S(1)}, f32[8,8,2,3,3,128]{5,1,4,3,2,0:T(8,128)}, u32[]{:S(2)}) copy-start(f32[8,8,2,3,3,128]{5,1,4,3,2,0:T(8,128)} %get-tuple-element.198) | copy-start | bytes 1769476
  748.9 159.2 %copy-start.5 = (f32[8,8,2,3,3,128]{5,1,4,3,2,0:T(8,128)S(1)}, f32[8,8,2,3,3,128]{5,1,4,3,2,0:T(8,128)}, u32[]{:S(2)}) copy-start(f32[8,8,2,3,3,128]{5,1,4,3,2,0:T(8,128)} %get-tuple-element.197) | copy-start | bytes 1769476
  749.0 159.1 %copy-start.4 = (f32[8,8,2,3,3,128]{5,1,4,3,2,0:T(8,128)S(1)}, f32[8,8,2,3,3,128]{5,1,4,3,2,0:T(8,128)}, u32[]{:S(2)}) copy-start(f32[8,8,2,3,3,128]{5,1,4,3,2,0:T(8,128)} %get-tuple-element.196) | copy-start | bytes 1769476
  749.0 14.9 %collective-permute-start.2 = (f32[8,2,2,3,3,128]{5,4,3,2,1,0:T(4,128)S(1)}, f32[8,2,2,3,3,128]{5,4,3,2,1,0:T(4,128)S(1)}, u32[]{:S(2)}, u32[]{:S(2)}) collective-permute-start(f32[8,2,2,3,3,128]{5,4,3,2,1,0:T(4,128)S(1)} %get-tuple-element.580), channel_id=1, source_target_pairs={{496,0},{0,16},{16,32},{32,48},{48,64},{64,80},{80,96},{96,112},{1... | collective-permute-start | bytes 442376 | tf_op jit(solution)/shard_map/while/body/eval_jaxpr/ppermute | solution.py:18
  763.9 13.1 %collective-permute-start.2 = (f32[8,2,2,3,3,128]{5,4,3,2,1,0:T(4,128)S(1)}, f32[8,2,2,3,3,128]{5,4,3,2,1,0:T(4,128)S(1)}, u32[]{:S(2)}, u32[]{:S(2)}) collective-permute-start(f32[8,2,2,3,3,128]{5,4,3,2,1,0:T(4,128)S(1)} %get-tuple-element.580), channel_id=1, source_target_pairs={{496,0},{0,16},{16,32},{32,48},{48,64},{64,80},{80,96},{96,112},{1... | collective-permute-start | bytes 442376 | tf_op jit(solution)/shard_map/while/body/eval_jaxpr/ppermute | solution.py:18
  777.1 13.0 %collective-permute-start.2 = (f32[8,2,2,3,3,128]{5,4,3,2,1,0:T(4,128)S(1)}, f32[8,2,2,3,3,128]{5,4,3,2,1,0:T(4,128)S(1)}, u32[]{:S(2)}, u32[]{:S(2)}) collective-permute-start(f32[8,2,2,3,3,128]{5,4,3,2,1,0:T(4,128)S(1)} %get-tuple-element.580), channel_id=1, source_target_pairs={{496,0},{0,16},{16,32},{32,48},{48,64},{64,80},{80,96},{96,112},{1... | collective-permute-start | bytes 442376 | tf_op jit(solution)/shard_map/while/body/eval_jaxpr/ppermute | solution.py:18
  790.2 13.0 %collective-permute-start.2 = (f32[8,2,2,3,3,128]{5,4,3,2,1,0:T(4,128)S(1)}, f32[8,2,2,3,3,128]{5,4,3,2,1,0:T(4,128)S(1)}, u32[]{:S(2)}, u32[]{:S(2)}) collective-permute-start(f32[8,2,2,3,3,128]{5,4,3,2,1,0:T(4,128)S(1)} %get-tuple-element.580), channel_id=1, source_target_pairs={{496,0},{0,16},{16,32},{32,48},{48,64},{64,80},{80,96},{96,112},{1... | collective-permute-start | bytes 442376 | tf_op jit(solution)/shard_map/while/body/eval_jaxpr/ppermute | solution.py:18
  803.3 13.0 %collective-permute-start.2 = (f32[8,2,2,3,3,128]{5,4,3,2,1,0:T(4,128)S(1)}, f32[8,2,2,3,3,128]{5,4,3,2,1,0:T(4,128)S(1)}, u32[]{:S(2)}, u32[]{:S(2)}) collective-permute-start(f32[8,2,2,3,3,128]{5,4,3,2,1,0:T(4,128)S(1)} %get-tuple-element.580), channel_id=1, source_target_pairs={{496,0},{0,16},{16,32},{32,48},{48,64},{64,80},{80,96},{96,112},{1... | collective-permute-start | bytes 442376 | tf_op jit(solution)/shard_map/while/body/eval_jaxpr/ppermute | solution.py:18
  816.4 13.0 %collective-permute-start.2 = (f32[8,2,2,3,3,128]{5,4,3,2,1,0:T(4,128)S(1)}, f32[8,2,2,3,3,128]{5,4,3,2,1,0:T(4,128)S(1)}, u32[]{:S(2)}, u32[]{:S(2)}) collective-permute-start(f32[8,2,2,3,3,128]{5,4,3,2,1,0:T(4,128)S(1)} %get-tuple-element.580), channel_id=1, source_target_pairs={{496,0},{0,16},{16,32},{32,48},{48,64},{64,80},{80,96},{96,112},{1... | collective-permute-start | bytes 442376 | tf_op jit(solution)/shard_map/while/body/eval_jaxpr/ppermute | solution.py:18
  829.5 13.0 %collective-permute-start.2 = (f32[8,2,2,3,3,128]{5,4,3,2,1,0:T(4,128)S(1)}, f32[8,2,2,3,3,128]{5,4,3,2,1,0:T(4,128)S(1)}, u32[]{:S(2)}, u32[]{:S(2)}) collective-permute-start(f32[8,2,2,3,3,128]{5,4,3,2,1,0:T(4,128)S(1)} %get-tuple-element.580), channel_id=1, source_target_pairs={{496,0},{0,16},{16,32},{32,48},{48,64},{64,80},{80,96},{96,112},{1... | collective-permute-start | bytes 442376 | tf_op jit(solution)/shard_map/while/body/eval_jaxpr/ppermute | solution.py:18
  842.6 13.0 %collective-permute-start.2 = (f32[8,2,2,3,3,128]{5,4,3,2,1,0:T(4,128)S(1)}, f32[8,2,2,3,3,128]{5,4,3,2,1,0:T(4,128)S(1)}, u32[]{:S(2)}, u32[]{:S(2)}) collective-permute-start(f32[8,2,2,3,3,128]{5,4,3,2,1,0:T(4,128)S(1)} %get-tuple-element.580), channel_id=1, source_target_pairs={{496,0},{0,16},{16,32},{32,48},{48,64},{64,80},{80,96},{96,112},{1... | collective-permute-start | bytes 442376 | tf_op jit(solution)/shard_map/while/body/eval_jaxpr/ppermute | solution.py:18
  855.7 13.0 %collective-permute-start.2 = (f32[8,2,2,3,3,128]{5,4,3,2,1,0:T(4,128)S(1)}, f32[8,2,2,3,3,128]{5,4,3,2,1,0:T(4,128)S(1)}, u32[]{:S(2)}, u32[]{:S(2)}) collective-permute-start(f32[8,2,2,3,3,128]{5,4,3,2,1,0:T(4,128)S(1)} %get-tuple-element.580), channel_id=1, source_target_pairs={{496,0},{0,16},{16,32},{32,48},{48,64},{64,80},{80,96},{96,112},{1... | collective-permute-start | bytes 442376 | tf_op jit(solution)/shard_map/while/body/eval_jaxpr/ppermute | solution.py:18
  868.8 13.0 %collective-permute-start.2 = (f32[8,2,2,3,3,128]{5,4,3,2,1,0:T(4,128)S(1)}, f32[8,2,2,3,3,128]{5,4,3,2,1,0:T(4,128)S(1)}, u32[]{:S(2)}, u32[]{:S(2)}) collective-permute-start(f32[8,2,2,3,3,128]{5,4,3,2,1,0:T(4,128)S(1)} %get-tuple-element.580), channel_id=1, source_target_pairs={{496,0},{0,16},{16,32},{32,48},{48,64},{64,80},{80,96},{96,112},{1... | collective-permute-start | bytes 442376 | tf_op jit(solution)/shard_map/while/body/eval_jaxpr/ppermute | solution.py:18
  881.9 13.0 %collective-permute-start.2 = (f32[8,2,2,3,3,128]{5,4,3,2,1,0:T(4,128)S(1)}, f32[8,2,2,3,3,128]{5,4,3,2,1,0:T(4,128)S(1)}, u32[]{:S(2)}, u32[]{:S(2)}) collective-permute-start(f32[8,2,2,3,3,128]{5,4,3,2,1,0:T(4,128)S(1)} %get-tuple-element.580), channel_id=1, source_target_pairs={{496,0},{0,16},{16,32},{32,48},{48,64},{64,80},{80,96},{96,112},{1... | collective-permute-start | bytes 442376 | tf_op jit(solution)/shard_map/while/body/eval_jaxpr/ppermute | solution.py:18
  895.0 13.0 %collective-permute-start.2 = (f32[8,2,2,3,3,128]{5,4,3,2,1,0:T(4,128)S(1)}, f32[8,2,2,3,3,128]{5,4,3,2,1,0:T(4,128)S(1)}, u32[]{:S(2)}, u32[]{:S(2)}) collective-permute-start(f32[8,2,2,3,3,128]{5,4,3,2,1,0:T(4,128)S(1)} %get-tuple-element.580), channel_id=1, source_target_pairs={{496,0},{0,16},{16,32},{32,48},{48,64},{64,80},{80,96},{96,112},{1... | collective-permute-start | bytes 442376 | tf_op jit(solution)/shard_map/while/body/eval_jaxpr/ppermute | solution.py:18
  (7 other events, 9.9 us)
